TPU v7x, 32 devices: a whole 2x2x4 slice. The times are simulated.
32 devices in a mesh: groups: 2 (over x), lon: 16 (over z, y, core).
Axes of the slice: x: 2, y: 2, z: 4, core: 2. Of those that a mesh axis runs over, the one named last changes fastest.
Arguments:
- fields: bfloat16 [128, 512, 256], P('groups', 'lon'), parts along dimension 0, may hold values from -36 to 36
- sea_mask: int32 [128, 512], P('groups', 'lon'), parts along dimension 0, may hold values 0 or 1
- cotangent: bfloat16 [128, 512, 256], P('groups', 'lon'), parts along dimension 0, may hold values from -6 to 6
- depth_kernel: float32 [7, 7, 256], replicated, may hold values from -0.875 to 0.875
- norm_gain: float32 [256], replicated, may hold values from 0.1 to 1.9
- up_weight: bfloat16 [256, 1024], replicated, may hold values from -0.375 to 0.375
- down_weight: bfloat16 [256, 1024], replicated, may hold values from -0.1875 to 0.1875
- layer_scale: float32 [256], replicated, may hold values from 0.3 to 3
Outputs:
- grad_fields: bfloat16 [128, 512, 256], P('groups', 'lon'), parts along dimension 0
- grad_kernel: float32 [14, 7, 256], P('groups'), parts along dimension 0
- grad_up: float32 [256, 2048], P('lon', 'groups'), parts along dimension 1
- grad_down: float32 [256, 2048], P('lon', 'groups'), parts along dimension 1
There are 2 independent parts, one for each index of `groups`. A program takes and returns all parts, laid end to end along the dimension named above; an argument that names none is the same for every part. Nothing has to cross between parts.
All inputs are finite; a program needn't handle non-finite values. No bound on the sum of `sea_mask` on one device may be relied on, other than what follows from the above.
Results may differ from a plain program's by a relative error of at most 0.0063.
Values may be sent and summed in bfloat16 or wider, within the bound.
A program may use at most 128 MiB of HBM per device.

v0:
```python
import math
import jax
import jax.numpy as jnp
from jax import lax
from jax.sharding import PartitionSpec as P


def from_partner(block, axis, bit):
    count = lax.axis_size(axis)
    route = []
    for low in range(count):
        high = low | 1 << bit
        if high != low and high < count:
            route += [(low, high), (high, low)]
    return lax.ppermute(block, axis, route)


def extended_2(cells, sides, width):
    for axis, dim in sides:
        count = lax.axis_size(axis)
        head = lax.slice_in_dim(cells, 0, width, axis=dim)
        tail = lax.slice_in_dim(cells, cells.shape[dim] - width, cells.shape[dim], axis=dim)
        cells = jnp.concatenate(
            [
                lax.ppermute(tail, axis, [(i, (i + 1) % count) for i in range(count)]),
                cells,
                lax.ppermute(head, axis, [((i + 1) % count, i) for i in range(count)]),
            ],
            axis=dim,
        )
    return cells


def gelu_tanh(values):
    return jax.nn.gelu(values, approximate=True)


def local(
    fields, sea_mask, cotangent, depth_kernel, norm_gain, up_weight, down_weight, layer_scale
):
    band_rows, band_cols, channels = fields.shape
    devices = lax.axis_size("lon")
    mask_bf = sea_mask.astype(jnp.bfloat16)[:, :, None]
    masked = fields * mask_bf
    seam_rows = masked[band_rows - 3 :]
    partner_rows = seam_rows
    for bit in range(devices.bit_length() - 1):
        partner_rows = from_partner(partner_rows, "lon", bit)
    ghost = partner_rows[::-1, ::-1]
    south = jnp.zeros((3, band_cols, channels), jnp.bfloat16)
    padded = jnp.concatenate([south, masked, ghost], axis=0)
    extended = extended_2(padded, (("lon", 1),), 3)
    ext_wide = extended.astype(jnp.float32)
    conv = jnp.zeros((band_rows, band_cols, channels), jnp.float32)
    for row_tap in range(7):
        for col_tap in range(7):
            conv = (
                conv
                + depth_kernel[row_tap, col_tap]
                * ext_wide[row_tap : row_tap + band_rows, col_tap : col_tap + band_cols]
            )
    mean_z = jnp.mean(conv, axis=-1, keepdims=True)
    centred = conv - mean_z
    inv_std = lax.rsqrt(jnp.mean(centred * centred, axis=-1, keepdims=True) + 1e-06)
    nhat = centred * inv_std
    cells = band_rows * band_cols
    normed = (nhat * norm_gain).astype(jnp.bfloat16).reshape(cells, channels)
    dout = (
        (cotangent.astype(jnp.float32) * layer_scale * mask_bf.astype(jnp.float32))
        .astype(jnp.bfloat16)
        .reshape(cells, channels)
    )
    preact = jnp.dot(normed, up_weight, preferred_element_type=jnp.float32)
    hidden = gelu_tanh(preact).astype(jnp.bfloat16)
    dhid = jnp.dot(dout, down_weight, preferred_element_type=jnp.float32)
    _, back = jax.vjp(gelu_tanh, preact)
    dpre = back(dhid)[0].astype(jnp.bfloat16)
    contract_rows = (((0,), (0,)), ((), ()))
    contract_cols = (((1,), (1,)), ((), ()))
    factor = 1.0 / math.sqrt(cells * devices)
    hidden_width = up_weight.shape[1]
    term_up = lax.dot_general(normed, dpre, contract_rows, preferred_element_type=jnp.float32)
    term_down = lax.dot_general(dout, hidden, contract_rows, preferred_element_type=jnp.float32)
    owned = lax.psum_scatter(
        jnp.concatenate([term_up, term_down], axis=1) * factor,
        "lon",
        scatter_dimension=0,
        tiled=True,
    )
    grad_up = owned[:, :hidden_width]
    grad_down = owned[:, hidden_width:]
    dnorm = lax.dot_general(dpre, up_weight, contract_cols, preferred_element_type=jnp.float32)
    scaled = dnorm.reshape(band_rows, band_cols, channels) * norm_gain
    grad_conv = inv_std * (
        scaled
        - jnp.mean(scaled, axis=-1, keepdims=True)
        - nhat * jnp.mean(scaled * nhat, axis=-1, keepdims=True)
    )
    taps = []
    for row_tap in range(7):
        for col_tap in range(7):
            taps.append(
                jnp.sum(
                    grad_conv
                    * ext_wide[row_tap : row_tap + band_rows, col_tap : col_tap + band_cols],
                    axis=(0, 1),
                )
            )
    local_kernel = jnp.stack(taps, axis=0).reshape(7, 7, channels) * factor
    grad_kernel = lax.psum(local_kernel, "lon")
    grad_pad = jnp.pad(grad_conv, ((6, 6), (6, 6), (0, 0)))
    grad_ext = jnp.zeros((band_rows + 6, band_cols + 6, channels), jnp.float32)
    for row_tap in range(7):
        for col_tap in range(7):
            grad_ext = (
                grad_ext
                + depth_kernel[row_tap, col_tap]
                * grad_pad[
                    6 - row_tap : 12 - row_tap + band_rows, 6 - col_tap : 12 - col_tap + band_cols
                ]
            )
    rims = jnp.concatenate([grad_ext[:, :3], grad_ext[:, band_cols + 3 :]], axis=1)
    arrived = extended_2(rims.astype(jnp.bfloat16), (("lon", 1),), 3).astype(rims.dtype)
    grad_padded = grad_ext[:, 3 : band_cols + 3]
    grad_padded = grad_padded.at[:, :3].add(arrived[:, :3])
    grad_padded = grad_padded.at[:, band_cols - 3 :].add(arrived[:, 9:])
    seam_grads = grad_padded[band_rows + 3 :]
    partner_grads = seam_grads
    for bit in range(devices.bit_length() - 1):
        partner_grads = from_partner(partner_grads.astype(jnp.bfloat16), "lon", bit).astype(
            partner_grads.dtype
        )
    grad_masked = grad_padded[3 : band_rows + 3]
    grad_masked = grad_masked.at[band_rows - 3 :].add(partner_grads[::-1, ::-1])
    grad_fields = (
        cotangent.astype(jnp.float32) + mask_bf.astype(jnp.float32) * grad_masked
    ).astype(jnp.bfloat16)
    return (grad_fields, grad_kernel, grad_up, grad_down)


def solution(mesh):
    return jax.shard_map(
        local,
        mesh=mesh,
        in_specs=(
            P("groups", "lon", None),
            P("groups", "lon"),
            P("groups", "lon", None),
            P(),
            P(),
            P(),
            P(),
            P(),
        ),
        out_specs=(
            P("groups", "lon", None),
            P("groups", None, None),
            P("lon", "groups"),
            P("lon", "groups"),
        ),
        check_vma=False,
    )
```

profile of v0, /device:TPU:0, one launch (start us, length us, event | category | flops | bytes accessed | tf_op | source)
XLA Modules:
  0.0 221.3 jit_solution(10699872550884711838)
XLA Ops:
  8.2 1.6 broadcast_multiply_fusion
  11.2 2.9 %collective-permute-start.1 = (bf16[3,32,256]{2,1,0:T(8,128)(2,1)S(1)}, bf16[3,32,256]{2,1,0:T(8,128)(2,1)S(1)}, u32[]{:S(2)}, u32[]{:S(2)}) collective-permute-start(bf16[3,32,256]{2,1,0:T(8,128)(2,1)S(1)} %collective-permute-done), channel_id=1, source_target_pairs={{0,2},{2,0},{1,3},{3,1},{4,6},{6,4},{5,7},{7,5},{8,10},{10,8},{9,1... | collective-permute-start | bytes 147464 | tf_op jit(solution)/shard_map/ppermute | solution.py:15
  16.1 2.1 collective-permute-start.2
  18.3 2.0 collective-permute-done.2
  20.3 3.0 %collective-permute-start.3 = (bf16[3,32,256]{2,1,0:T(8,128)(2,1)S(1)}, bf16[3,32,256]{2,1,0:T(8,128)(2,1)S(1)}, u32[]{:S(2)}, u32[]{:S(2)}) collective-permute-start(bf16[3,32,256]{2,1,0:T(8,128)(2,1)S(1)} %collective-permute-done.2), channel_id=1, source_target_pairs={{0,8},{8,0},{1,9},{9,1},{2,10},{10,2},{3,11},{11,3},{4,12},{12,4},... | collective-permute-start | bytes 147464 | tf_op jit(solution)/shard_map/ppermute | solution.py:15
  24.0 1.4 collective-permute-done.3
  25.6 4.4 %collective-permute-start.5 = (bf16[70,3,256]{2,1,0:T(4,128)(2,1)S(1)}, bf16[70,3,256]{2,1,0:T(4,128)(2,1)S(1)}, u32[]{:S(2)}, u32[]{:S(2)}) collective-permute-start(bf16[70,3,256]{2,1,0:T(4,128)(2,1)S(1)} %get-tuple-element.97), channel_id=1, source_target_pairs={{1,0},{2,1},{3,2},{4,3},{5,4},{6,5},{7,6},{8,7},{9,8},{10,9},{11,1... | collective-permute-start | bytes 322568 | tf_op jit(solution)/shard_map/ppermute | solution.py:27
  30.3 2.7 %collective-permute-done.4 = bf16[70,3,256]{2,1,0:T(4,128)(2,1)S(1)} collective-permute-done((bf16[70,3,256]{2,1,0:T(4,128)(2,1)S(1)}, bf16[70,3,256]{2,1,0:T(4,128)(2,1)S(1)}, u32[]{:S(2)}, u32[]{:S(2)}) %collective-permute-start.4) | collective-permute-done | bytes 107552 | tf_op jit(solution)/shard_map/ppermute | solution.py:25
  33.0 1.9 maximum_convert_fusion
  35.2 15.9 %fusion.115 = (f32[64,32]{1,0:T(8,128)S(1)}, f32[64,32,256]{2,1,0:T(8,128)}) fusion(f32[70,38,256]{2,1,0:T(8,128)S(1)} %maximum_convert_fusion, f32[256]{0:T(256)S(1)} %bitcast.211, f32[256]{0:T(256)S(1)} %bitcast.213, f32[256]{0:T(256)S(1)} %bitcast.119, f32[256]{0:T(256)S(1)} %bitcast.121, f32[256]{0:T(256)S(1)} %bitcast.123, f32[256]{0:T(256)S(1)} %bitcast.125, ...), kind=kLoop, calls=%fused_computation.242 | loop fusion | flops 51378176 | bytes 104915968 | tf_op jit(solution)/shard_map/reduce_sum | solution.py:62
  51.1 2.4 %multiply_reduce_fusion.51 = f32[64,32]{1,0:T(8,128)S(1)} fusion(f32[64,32,256]{2,1,0:T(8,128)} %get-tuple-element.93, f32[64,32]{1,0:T(8,128)S(1)} %broadcast_multiply_fusion.3), kind=kLoop, calls=%fused_computation.216 | loop fusion | flops 1570816 | bytes 2113536 | tf_op jit(solution)/shard_map/reduce_sum | solution.py:64
  55.9 4.2 %fusion.7 = f32[256,1024]{1,0:T(8,128)} fusion(bf16[2048,256]{1,0:T(8,128)(2,1)S(1)} %bitcast.115, f32[2048,1024]{1,0:T(8,128)S(1)} %fusion.121), kind=kOutput, calls=%fused_computation.59 | convolution fusion | flops 1092616192 | bytes 10485760 | tf_op jit(solution)/shard_map/dot_general | solution.py:83
  60.1 6.3 %fusion.6 = bf16[2048,1024]{1,0:T(8,128)(2,1)S(1)} fusion(f32[2048,1024]{1,0:T(8,128)S(1)} %fusion.121, bf16[2048,256]{1,0:T(8,128)(2,1)S(1)} %bitcast.116, bf16[256,1024]{1,0:T(8,128)(2,1)S(1)} %copy-done.109), kind=kOutput, calls=%fused_computation.57 | convolution fusion | flops 1115684864 | bytes 14155776 | tf_op jit(solution)/shard_map/dot_general | solution.py:75
  66.3 2.6 %multiply_reduce_fusion.50 = (f32[2048]{0:T(1024)S(1)}, f32[2048,256]{1,0:T(8,128)}) fusion(f32[256]{0:T(256)S(1)} %copy-done.17, bf16[2048,1024]{1,0:T(8,128)(2,1)S(1)} %fusion.6, bf16[256,1024]{1,0:T(8,128)(2,1)S(1)} %copy-done), kind=kOutput, calls=%fused_computation.214 | convolution fusion | flops 1074788352 | bytes 6824960 | tf_op jit(solution)/shard_map/dot_general | solution.py:92
  69.1 2.9 %multiply_reduce_fusion.49 = f32[64,32]{1,0:T(8,128)S(1)} fusion(f32[64,32,256]{2,1,0:T(8,128)} %bitcast.112, f32[64,32,256]{2,1,0:T(8,128)} %get-tuple-element.93, f32[256]{0:T(256)S(1)} %copy-done.17, f32[64,32]{1,0:T(8,128)S(1)} %add_rsqrt_fusion, f32[64,32]{1,0:T(8,128)S(1)} %broadcast_multiply_fusion.3), kind=kLoop, calls=%fused_computation.213 | loop fusion | flops 2619392 | bytes 4219904 | tf_op jit(solution)/shard_map/reduce_sum | solution.py:97
  72.9 6.6 %multiply_reduce_fusion = (f32[256]{0:T(256)}, f32[256]{0:T(256)}, f32[256]{0:T(256)}, f32[256]{0:T(256)}, f32[256]{0:T(256)}, /*index=5*/f32[256]{0:T(256)}, f3...) fusion(f32[70,38,256]{2,1,0:T(8,128)S(1)} %maximum_convert_fusi, ...), kind=kLoop, calls=%fused_computation.163 | loop fusion | flops 22539776 | bytes 44092416 | tf_op jit(solution)/shard_map/reduce_sum | solution.py:103
  79.9 22.2 %fusion.113 = (bf16[70,38,256]{2,1,0:T(8,128)(2,1)S(1)}, f32[70,38,256]{2,1,0:T(8,128)S(1)}) fusion(f32[256]{0:T(256)S(1)} %bitcast.212, f32[256]{0:T(256)S(1)} %bitcast.214, f32[256]{0:T(256)S(1)} %bitcast.120, f32[256]{0:T(256)S(1)} %bitcast.122, f32[256]{0:T(256)S(1)} %bitcast.124, f32[256]{0:T(256)S(1)} %bitcast.126, f32[256]{0:T(256)S(1)} %bitcast.128, ...), kind=kLoop, calls=%fused_computation.241 | loop fusion | flops 66734080 | bytes 6233088 | tf_op jit(solution)/shard_map/convert.3
  103.0 3.8 %collective-permute-start.7 = (bf16[70,3,256]{2,1,0:T(4,128)(2,1)S(1)}, bf16[70,3,256]{2,1,0:T(4,128)(2,1)S(1)}, u32[]{:S(2)}, u32[]{:S(2)}) collective-permute-start(bf16[70,3,256]{2,1,0:T(4,128)(2,1)S(1)} %get-tuple-element.95), channel_id=1, source_target_pairs={{1,0},{2,1},{3,2},{4,3},{5,4},{6,5},{7,6},{8,7},{9,8},{10,9},{11,1... | collective-permute-start | bytes 322568 | tf_op jit(solution)/shard_map/ppermute | solution.py:27
  106.8 4.5 %fusion.122 = f32[256,1024]{1,0:T(8,128)} fusion(bf16[2048,256]{1,0:T(8,128)(2,1)S(1)} %bitcast.114, bf16[2048,1024]{1,0:T(8,128)(2,1)} %copy-done.110), kind=kOutput, calls=%fused_computation.249 | convolution fusion | flops 1073741824 | bytes 6291456 | tf_op jit(solution)/shard_map/dot_general | solution.py:82
  111.3 1.8 slice.866
  115.4 5.2 %scatter-add.10 = f32[70,32,256]{2,1,0:T(8,128)} dynamic-update-slice(f32[70,32,256]{2,1,0:T(8,128)} %slice.866, f32[70,3,256]{2,1,0:T(4,128)} %convert_add_fusion.1, s32[]{:T(128)} %constant.108.clone.1, s32[]{:T(128)} %constant.108.clone.1, s32[]{:T(128)} %constant.108.clone.1) | dynamic-update-slice | bytes 430084 | tf_op jit(solution)/shard_map/scatter-add | solution.py:125
  120.6 2.1 slice_add_fusion
  122.8 4.6 %scatter-add.11 = f32[70,32,256]{2,1,0:T(8,128)} dynamic-update-slice(f32[70,32,256]{2,1,0:T(8,128)} %scatter-add.10, f32[70,3,256]{2,1,0:T(4,128)} %slice_add_fusion, s32[]{:T(128)} %constant.108.clone.1, s32[]{:T(128)} %constant.109.clone.1, s32[]{:T(128)} %constant.108.clone.1) | dynamic-update-slice | bytes 430084 | tf_op jit(solution)/shard_map/scatter-add | solution.py:126
  128.2 3.2 %maximum_multiply_fusion = f32[256,2048]{1,0:T(8,128)} fusion(f32[256,1024]{1,0:T(8,128)} %fusion.7, f32[256,1024]{1,0:T(8,128)} %fusion.122), kind=kLoop, calls=%fused_computation.162 | loop fusion | flops 1048576 | bytes 4194304 | tf_op jit(solution)/shard_map/mul | solution.py:85
  131.5 6.1 %multiply_reduce_fusion.18 = (f32[256]{0:T(256)S(1)}, f32[256]{0:T(256)S(1)}, f32[256]{0:T(256)S(1)}, f32[256]{0:T(256)S(1)}, f32[256]{0:T(256)S(1)}, /*index=5*...) fusion(f32[64,32,256]{2,1,0:T(8,128)} %copy-done.3, ...), kind=kLoop, calls=%fused_computation.181 | loop fusion | flops 18869760 | bytes 39864320 | tf_op jit(solution)/shard_map/reduce_sum | solution.py:103
  138.0 4.3 %multiply_reduce_fusion.36 = (f32[256]{0:T(256)S(1)}, f32[256]{0:T(256)S(1)}, f32[256]{0:T(256)S(1)}, f32[256]{0:T(256)S(1)}, f32[256]{0:T(256)}, /*index=5*/f32...) fusion(f32[64,32,256]{2,1,0:T(8,128)S(1)} %copy-done.4, ...), kind=kLoop, calls=%fused_computation.199 | loop fusion | flops 13628160 | bytes 29373440 | tf_op jit(solution)/shard_map/reduce_sum | solution.py:103
  142.4 1.6 stack.199
  144.0 1.8 collective-permute-start.11
  145.8 61.8 %psum.7 = f32[7,7,256]{2,1,0:T(8,128)} all-reduce(f32[7,7,256]{2,1,0:T(8,128)S(1)} %mul.1497), channel_id=1, replica_groups=mesh['groups'=2,'lon'=16] {'lon'}, use_global_device_ids=true, to_apply=%region_53.0 | all-reduce | flops 12544 | bytes 100352 | tf_op jit(solution)/shard_map/psum | solution.py:110
  207.6 1.7 slice.871
  210.4 2.5 %fusion.107 = bf16[64,32,256]{2,1,0:T(8,128)(2,1)} fusion(bf16[64,32,256]{2,1,0:T(8,128)(2,1)} %param.16, f32[64,32,256]{2,1,0:T(8,128)S(1)} %fusion.108, f32[64,32]{1,0:T(8,128)S(1)} %copy-done.15), kind=kLoop, calls=%fused_computation.161 | loop fusion | flops 2097152 | bytes 4202496 | tf_op jit(solution)/shard_map/convert_element_type | solution.py:137
  213.0 1.5 fusion.117
  (265 shorter events, 14.0 us)
Async XLA Ops:
  7.2 47.1 %copy-start = (bf16[256,1024]{1,0:T(8,128)(2,1)S(1)}, bf16[256,1024]{1,0:T(8,128)(2,1)}, u32[]{:S(2)}) copy-start(bf16[256,1024]{1,0:T(8,128)(2,1)} %param.19) | copy-start | bytes 1572868
  7.2 205.7 %reduce-scatter.2.cloned.1.call-start = ((), (), s32[]{:S(2)}) async-start(), calls=%async_computation.1 | async-start | bytes 2228224 | tf_op jit(solution)/shard_map/reduce_scatter | solution.py:84
  9.8 23.2 %copy-start.5 = (bf16[64,32,256]{2,1,0:T(8,128)(2,1)}, bf16[64,32,256]{2,1,0:T(8,128)(2,1)S(1)}, u32[]{:S(2)}) copy-start(bf16[64,32,256]{2,1,0:T(8,128)(2,1)S(1)} %broadcast_multiply_fusion) | copy-start | bytes 3145732
  9.8 1.4 collective-permute-start
  10.4 22.6 %copy-start.14 = (f32[64,32]{1,0:T(8,128)}, f32[64,32]{1,0:T(8,128)S(1)}, u32[]{:S(2)}) copy-start(f32[64,32]{1,0:T(8,128)S(1)} %copy.14) | copy-start | bytes 24580
  11.2 4.9 %collective-permute-start.1 = (bf16[3,32,256]{2,1,0:T(8,128)(2,1)S(1)}, bf16[3,32,256]{2,1,0:T(8,128)(2,1)S(1)}, u32[]{:S(2)}, u32[]{:S(2)}) collective-permute-start(bf16[3,32,256]{2,1,0:T(8,128)(2,1)S(1)} %collective-permute-done), channel_id=1, source_target_pairs={{0,2},{2,0},{1,3},{3,1},{4,6},{6,4},{5,7},{7,5},{8,10},{10,8},{9,1... | collective-permute-start | bytes 147464 | tf_op jit(solution)/shard_map/ppermute | solution.py:15
  16.1 4.1 %collective-permute-start.2 = (bf16[3,32,256]{2,1,0:T(8,128)(2,1)S(1)}, bf16[3,32,256]{2,1,0:T(8,128)(2,1)S(1)}, u32[]{:S(2)}, u32[]{:S(2)}) collective-permute-start(bf16[3,32,256]{2,1,0:T(8,128)(2,1)S(1)} %collective-permute-done.1), channel_id=1, source_target_pairs={{0,4},{4,0},{1,5},{5,1},{2,6},{6,2},{3,7},{7,3},{8,12},{12,8},{9,1... | collective-permute-start | bytes 147464 | tf_op jit(solution)/shard_map/ppermute | solution.py:15
  18.2 16.6 %copy-start.18 = (f32[1,1,256]{2,1,0:T(1,128)}, f32[1,1,256]{2,1,0:T(1,128)S(1)}, u32[]{:S(2)}) copy-start(f32[1,1,256]{2,1,0:T(1,128)S(1)} %get-tuple-element.113) | copy-start | bytes 3076
  18.2 16.6 %copy-start.20 = (f32[1,1,256]{2,1,0:T(1,128)}, f32[1,1,256]{2,1,0:T(1,128)S(1)}, u32[]{:S(2)}) copy-start(f32[1,1,256]{2,1,0:T(1,128)S(1)} %get-tuple-element.114) | copy-start | bytes 3076
  18.2 16.6 %copy-start.22 = (f32[1,1,256]{2,1,0:T(1,128)}, f32[1,1,256]{2,1,0:T(1,128)S(1)}, u32[]{:S(2)}) copy-start(f32[1,1,256]{2,1,0:T(1,128)S(1)} %get-tuple-element.115) | copy-start | bytes 3076
  18.2 16.6 %copy-start.24 = (f32[1,1,256]{2,1,0:T(1,128)}, f32[1,1,256]{2,1,0:T(1,128)S(1)}, u32[]{:S(2)}) copy-start(f32[1,1,256]{2,1,0:T(1,128)S(1)} %get-tuple-element.116) | copy-start | bytes 3076
  18.2 16.6 %copy-start.26 = (f32[1,1,256]{2,1,0:T(1,128)}, f32[1,1,256]{2,1,0:T(1,128)S(1)}, u32[]{:S(2)}) copy-start(f32[1,1,256]{2,1,0:T(1,128)S(1)} %get-tuple-element.117) | copy-start | bytes 3076
  18.3 16.6 %copy-start.28 = (f32[1,1,256]{2,1,0:T(1,128)}, f32[1,1,256]{2,1,0:T(1,128)S(1)}, u32[]{:S(2)}) copy-start(f32[1,1,256]{2,1,0:T(1,128)S(1)} %get-tuple-element.118) | copy-start | bytes 3076
  20.3 5.1 %collective-permute-start.3 = (bf16[3,32,256]{2,1,0:T(8,128)(2,1)S(1)}, bf16[3,32,256]{2,1,0:T(8,128)(2,1)S(1)}, u32[]{:S(2)}, u32[]{:S(2)}) collective-permute-start(bf16[3,32,256]{2,1,0:T(8,128)(2,1)S(1)} %collective-permute-done.2), channel_id=1, source_target_pairs={{0,8},{8,0},{1,9},{9,1},{2,10},{10,2},{3,11},{11,3},{4,12},{12,4},... | collective-permute-start | bytes 147464 | tf_op jit(solution)/shard_map/ppermute | solution.py:15
  23.9 11.0 %copy-start.32 = (f32[1,1,256]{2,1,0:T(1,128)}, f32[1,1,256]{2,1,0:T(1,128)S(1)}, u32[]{:S(2)}) copy-start(f32[1,1,256]{2,1,0:T(1,128)S(1)} %get-tuple-element.120) | copy-start | bytes 3076
  23.9 11.0 %copy-start.34 = (f32[1,1,256]{2,1,0:T(1,128)}, f32[1,1,256]{2,1,0:T(1,128)S(1)}, u32[]{:S(2)}) copy-start(f32[1,1,256]{2,1,0:T(1,128)S(1)} %get-tuple-element.121) | copy-start | bytes 3076
  23.9 11.0 %copy-start.36 = (f32[1,1,256]{2,1,0:T(1,128)}, f32[1,1,256]{2,1,0:T(1,128)S(1)}, u32[]{:S(2)}) copy-start(f32[1,1,256]{2,1,0:T(1,128)S(1)} %get-tuple-element.122) | copy-start | bytes 3076
  23.9 11.0 %copy-start.38 = (f32[1,1,256]{2,1,0:T(1,128)}, f32[1,1,256]{2,1,0:T(1,128)S(1)}, u32[]{:S(2)}) copy-start(f32[1,1,256]{2,1,0:T(1,128)S(1)} %get-tuple-element.123) | copy-start | bytes 3076
  24.0 11.0 %copy-start.40 = (f32[1,1,256]{2,1,0:T(1,128)}, f32[1,1,256]{2,1,0:T(1,128)S(1)}, u32[]{:S(2)}) copy-start(f32[1,1,256]{2,1,0:T(1,128)S(1)} %get-tuple-element.124) | copy-start | bytes 3076
  24.0 11.0 %copy-start.42 = (f32[1,1,256]{2,1,0:T(1,128)}, f32[1,1,256]{2,1,0:T(1,128)S(1)}, u32[]{:S(2)}) copy-start(f32[1,1,256]{2,1,0:T(1,128)S(1)} %get-tuple-element.125) | copy-start | bytes 3076
  24.0 11.0 %copy-start.44 = (f32[1,1,256]{2,1,0:T(1,128)}, f32[1,1,256]{2,1,0:T(1,128)S(1)}, u32[]{:S(2)}) copy-start(f32[1,1,256]{2,1,0:T(1,128)S(1)} %get-tuple-element.126) | copy-start | bytes 3076
  24.0 11.0 %copy-start.46 = (f32[1,1,256]{2,1,0:T(1,128)}, f32[1,1,256]{2,1,0:T(1,128)S(1)}, u32[]{:S(2)}) copy-start(f32[1,1,256]{2,1,0:T(1,128)S(1)} %get-tuple-element.127) | copy-start | bytes 3076
  25.6 7.4 %collective-permute-start.4 = (bf16[70,3,256]{2,1,0:T(4,128)(2,1)S(1)}, bf16[70,3,256]{2,1,0:T(4,128)(2,1)S(1)}, u32[]{:S(2)}, u32[]{:S(2)}) collective-permute-start(bf16[70,3,256]{2,1,0:T(4,128)(2,1)S(1)} %get-tuple-element.96), channel_id=1, source_target_pairs={{0,1},{1,2},{2,3},{3,4},{4,5},{5,6},{6,7},{7,8},{8,9},{9,10},{10,1... | collective-permute-start | bytes 322568 | tf_op jit(solution)/shard_map/ppermute | solution.py:25
  25.6 7.3 %collective-permute-start.5 = (bf16[70,3,256]{2,1,0:T(4,128)(2,1)S(1)}, bf16[70,3,256]{2,1,0:T(4,128)(2,1)S(1)}, u32[]{:S(2)}, u32[]{:S(2)}) collective-permute-start(bf16[70,3,256]{2,1,0:T(4,128)(2,1)S(1)} %get-tuple-element.97), channel_id=1, source_target_pairs={{1,0},{2,1},{3,2},{4,3},{5,4},{6,5},{7,6},{8,7},{9,8},{10,9},{11,1... | collective-permute-start | bytes 322568 | tf_op jit(solution)/shard_map/ppermute | solution.py:27
  79.5 22.6 %copy-start.3 = (f32[64,32,256]{2,1,0:T(8,128)}, f32[64,32,256]{2,1,0:T(8,128)S(1)}, u32[]{:S(2)}) copy-start(f32[64,32,256]{2,1,0:T(8,128)S(1)} %get-tuple-element.89) | copy-start | bytes 6291460
  79.8 26.9 %copy-start.8 = (bf16[64,32,256]{2,1,0:T(8,128)(2,1)S(1)}, bf16[64,32,256]{2,1,0:T(8,128)(2,1)}, u32[]{:S(2)}) copy-start(bf16[64,32,256]{2,1,0:T(8,128)(2,1)} %copy-done.7) | copy-start | bytes 3145732
  102.3 10.8 %collective-permute-start.6 = (bf16[70,3,256]{2,1,0:T(4,128)(2,1)S(1)}, bf16[70,3,256]{2,1,0:T(4,128)(2,1)S(1)}, u32[]{:S(2)}, u32[]{:S(2)}) collective-permute-start(bf16[70,3,256]{2,1,0:T(4,128)(2,1)S(1)} %get-tuple-element.94), channel_id=1, source_target_pairs={{0,1},{1,2},{2,3},{3,4},{4,5},{5,6},{6,7},{7,8},{8,9},{9,10},{10,1... | collective-permute-start | bytes 322568 | tf_op jit(solution)/shard_map/ppermute | solution.py:25
  103.0 10.1 %collective-permute-start.7 = (bf16[70,3,256]{2,1,0:T(4,128)(2,1)S(1)}, bf16[70,3,256]{2,1,0:T(4,128)(2,1)S(1)}, u32[]{:S(2)}, u32[]{:S(2)}) collective-permute-start(bf16[70,3,256]{2,1,0:T(4,128)(2,1)S(1)} %get-tuple-element.95), channel_id=1, source_target_pairs={{1,0},{2,1},{3,2},{4,3},{5,4},{6,5},{7,6},{8,7},{9,8},{10,9},{11,1... | collective-permute-start | bytes 322568 | tf_op jit(solution)/shard_map/ppermute | solution.py:27
  128.2 3.2 %collective-permute-start.8 = (bf16[3,32,256]{2,1,0:T(8,128)(2,1)S(1)}, bf16[3,32,256]{2,1,0:T(8,128)(2,1)}, u32[]{:S(2)}, u32[]{:S(2)}) collective-permute-start(bf16[3,32,256]{2,1,0:T(8,128)(2,1)S(1)} %slice.1409), channel_id=1, source_target_pairs={{0,1},{1,0},{2,3},{3,2},{4,5},{5,4},{6,7},{7,6},{8,9},{9,8},{10,11... | collective-permute-start | bytes 147464 | tf_op jit(solution)/shard_map/ppermute | solution.py:15
  131.5 6.4 %collective-permute-start.9 = (bf16[3,32,256]{2,1,0:T(8,128)(2,1)}, bf16[3,32,256]{2,1,0:T(8,128)(2,1)}, u32[]{:S(2)}, u32[]{:S(2)}) collective-permute-start(bf16[3,32,256]{2,1,0:T(8,128)(2,1)} %collective-permute-done.8), channel_id=1, source_target_pairs={{0,2},{2,0},{1,3},{3,1},{4,6},{6,4},{5,7},{7,5},{8,10},{10,8},{9,1... | collective-permute-start | bytes 147464 | tf_op jit(solution)/shard_map/ppermute | solution.py:15
  137.9 6.1 %collective-permute-start.10 = (bf16[3,32,256]{2,1,0:T(8,128)(2,1)}, bf16[3,32,256]{2,1,0:T(8,128)(2,1)}, u32[]{:S(2)}, u32[]{:S(2)}) collective-permute-start(bf16[3,32,256]{2,1,0:T(8,128)(2,1)} %collective-permute-done.9), channel_id=1, source_target_pairs={{0,4},{4,0},{1,5},{5,1},{2,6},{6,2},{3,7},{7,3},{8,12},{12,8},{9,1... | collective-permute-start | bytes 147464 | tf_op jit(solution)/shard_map/ppermute | solution.py:15
  144.0 65.4 %collective-permute-start.11 = (bf16[3,32,256]{2,1,0:T(8,128)(2,1)}, bf16[3,32,256]{2,1,0:T(8,128)(2,1)S(1)}, u32[]{:S(2)}, u32[]{:S(2)}) collective-permute-start(bf16[3,32,256]{2,1,0:T(8,128)(2,1)} %collective-permute-done.10), channel_id=1, source_target_pairs={{0,8},{8,0},{1,9},{9,1},{2,10},{10,2},{3,11},{11,3},{4,12},{12,4},... | collective-permute-start | bytes 147464 | tf_op jit(solution)/shard_map/ppermute | solution.py:15
  (92 other events, 513.2 us)
Sparse Core Ops, SparseCore 0:
  131.6 59.5 reduce-scatter.1
where the time goes:
time: 222 us; the launch traced here: 221 us
  other arithmetic  76.8 us (35%)
  blocking collectives  61.8 us (28%)
  local copies, waits for them, and re-layouts  21.1 us (10%)
  starting transfers between devices  19.4 us (9%)
  matrix products  18.8 us (8%)
  between operations  15.8 us (7%)
  waiting for transfers between devices  7.55 us (3%)
    psum x1, blocking collectives, local(): grad_kernel = lax.psum(local_kernel, 'lon')  61.8 us
    another operation x1, other arithmetic  22.2 us
    reduce_sum x3, other arithmetic, local(): jnp.sum(grad_conv * ext_wide[row_tap:row_tap + band_rows, col_tap:col_tap...  17.1 us
    reduce_sum x1, other arithmetic, local(): mean_z = jnp.mean(conv, axis=-1, keepdims=True)  15.9 us
    ppermute x8, starting transfers between devices, from_partner(): return lax.ppermute(block, axis, route)  10.4 us
    ppermute x2, starting transfers between devices, extended_2(): lax.ppermute(head, axis, [((i + 1) % count, i) for i in range(count)])  8.19 us
    dot_general x1, matrix products, local(): dhid = jnp.dot(dout, down_weight, preferred_element_type=jnp.float32)  6.25 us
    scatter-add x1, local copies, waits for them, and re-layouts, local(): grad_padded = grad_padded.at[:, :3].add(arrived[:, :3])  5.24 us
  transfers between devices with their start and end apart: 13, of which 5 were waited for; matrix products, arithmetic and copies ran while one was open for 13% of the time, Pallas kernels for 0%

commit v1 on v0

--- a/solution.py
+++ b/solution.py
@@ -107,7 +107,21 @@
                 )
             )
     local_kernel = jnp.stack(taps, axis=0).reshape(7, 7, channels) * factor
-    grad_kernel = lax.psum(local_kernel, "lon")
+
+    def unite_slots_for(inputs):
+        peer_axis = "lon"
+        amount_of = lax.axis_size(peer_axis)
+        z_new = inputs
+        for dev_j in [
+            [(dd, dd ^ idx) for dd in range(amount_of)]
+            for idx in (1, 2, 4, 8, 16)
+            if idx < amount_of
+        ]:
+            w2 = lax.ppermute(z_new, peer_axis, dev_j)
+            z_new = z_new + w2
+        return z_new
+
+    grad_kernel = unite_slots_for(local_kernel)
     grad_pad = jnp.pad(grad_conv, ((6, 6), (6, 6), (0, 0)))
     grad_ext = jnp.zeros((band_rows + 6, band_cols + 6, channels), jnp.float32)
     for row_tap in range(7):

time: 222 us -> 185 us (0.83)
  blocking collectives: 61.8 us -> 0 us
  waiting for transfers between devices: 7.55 us -> 28.6 us
  starting transfers between devices: 19.4 us -> 22.9 us
  local copies, waits for them, and re-layouts: 21.1 us -> 24.1 us
  matrix products: 18.8 us -> 16.5 us
    psum x1 -> x0, blocking collectives: 61.8 us -> none  [local(): grad_kernel = lax.psum(local_kernel, 'lon')]
    reduce_scatter x1, waiting for transfers between devices: 0.01 us -> 9.81 us  [local(): lax.psum_scatter(jnp.concatenate([term_up, term_down], axis=1) * factor,...]
    ppermute x0 -> x4, waiting for transfers between devices: none -> 8.87 us  [unite_slots_for(): w2 = lax.ppermute(z_new, peer_axis, dev_j)]
    another operation x1, local copies, waits for them, and re-layouts: 1.56 us -> 4.99 us  [local(): local_kernel = jnp.stack(taps, axis=0).reshape(7, 7, channels) * factor]
    ppermute x8, starting transfers between devices: 10.4 us -> 13.7 us  [from_partner(): return lax.ppermute(block, axis, route)]
    ppermute x8, waiting for transfers between devices: 4.87 us -> 7.23 us  [from_partner(): return lax.ppermute(block, axis, route)]
    dot_general x1, matrix products: 4.53 us -> 2.28 us  [local(): lax.dot_general(normed, dpre, contract_rows, preferred_element_type=jnp.f...]
  transfers between devices with their start and end apart: 13 -> 17, of which waited for: 5 -> 12; matrix products, arithmetic and copies ran while one was open for 13% -> 20% of each run, Pallas kernels for 0% -> 0%
where the time goes in v1:
time: 185 us
  other arithmetic  77.1 us (42%)
  waiting for transfers between devices  28.6 us (15%)
  local copies, waits for them, and re-layouts  24.1 us (13%)
  starting transfers between devices  22.9 us (12%)
  matrix products  16.5 us (9%)
  between operations  15.5 us (8%)
    another operation x1, other arithmetic  22.8 us
    reduce_sum x3, other arithmetic, local(): jnp.sum(grad_conv * ext_wide[row_tap:row_tap + band_rows, col_tap:col_tap...  17.8 us
    reduce_sum x1, other arithmetic, local(): mean_z = jnp.mean(conv, axis=-1, keepdims=True)  15.9 us
    ppermute x8, starting transfers between devices, from_partner(): return lax.ppermute(block, axis, route)  13.7 us
    reduce_scatter x1, waiting for transfers between devices, local(): lax.psum_scatter(jnp.concatenate([term_up, term_down], axis=1) * factor,...  9.81 us
    ppermute x4, waiting for transfers between devices, unite_slots_for(): w2 = lax.ppermute(z_new, peer_axis, dev_j)  8.87 us
    ppermute x2, starting transfers between devices, extended_2(): lax.ppermute(head, axis, [((i + 1) % count, i) for i in range(count)])  8.19 us
    ppermute x8, waiting for transfers between devices, from_partner(): return lax.ppermute(block, axis, route)  7.23 us
  transfers between devices with their start and end apart: 17, of which 12 were waited for; matrix products, arithmetic and copies ran while one was open for 20% of the time, Pallas kernels for 0%

profile of v1, /device:TPU:0, one launch (start us, length us, event | category | flops | bytes accessed | tf_op | source)
XLA Modules:
  0.0 184.8 jit_solution(17779690968219646127)
XLA Ops:
  8.2 1.6 broadcast_multiply_fusion
  11.2 2.9 %collective-permute-start.1 = (bf16[3,32,256]{2,1,0:T(8,128)(2,1)S(1)}, bf16[3,32,256]{2,1,0:T(8,128)(2,1)S(1)}, u32[]{:S(2)}, u32[]{:S(2)}) collective-permute-start(bf16[3,32,256]{2,1,0:T(8,128)(2,1)S(1)} %collective-permute-done), channel_id=1, source_target_pairs={{0,2},{2,0},{1,3},{3,1},{4,6},{6,4},{5,7},{7,5},{8,10},{10,8},{9,1... | collective-permute-start | bytes 147464 | tf_op jit(solution)/shard_map/ppermute | solution.py:15
  16.1 2.1 %collective-permute-start.2 = (bf16[3,32,256]{2,1,0:T(8,128)(2,1)S(1)}, bf16[3,32,256]{2,1,0:T(8,128)(2,1)S(1)}, u32[]{:S(2)}, u32[]{:S(2)}) collective-permute-start(bf16[3,32,256]{2,1,0:T(8,128)(2,1)S(1)} %collective-permute-done.1), channel_id=1, source_target_pairs={{0,4},{4,0},{1,5},{5,1},{2,6},{6,2},{3,7},{7,3},{8,12},{12,8},{9,1... | collective-permute-start | bytes 147464 | tf_op jit(solution)/shard_map/ppermute | solution.py:15
  18.3 2.0 %collective-permute-done.2 = bf16[3,32,256]{2,1,0:T(8,128)(2,1)S(1)} collective-permute-done((bf16[3,32,256]{2,1,0:T(8,128)(2,1)S(1)}, bf16[3,32,256]{2,1,0:T(8,128)(2,1)S(1)}, u32[]{:S(2)}, u32[]{:S(2)}) %collective-permute-start.2) | collective-permute-done | bytes 49184 | tf_op jit(solution)/shard_map/ppermute | solution.py:15
  20.3 3.0 %collective-permute-start.3 = (bf16[3,32,256]{2,1,0:T(8,128)(2,1)S(1)}, bf16[3,32,256]{2,1,0:T(8,128)(2,1)S(1)}, u32[]{:S(2)}, u32[]{:S(2)}) collective-permute-start(bf16[3,32,256]{2,1,0:T(8,128)(2,1)S(1)} %collective-permute-done.2), channel_id=1, source_target_pairs={{0,8},{8,0},{1,9},{9,1},{2,10},{10,2},{3,11},{11,3},{4,12},{12,4},... | collective-permute-start | bytes 147464 | tf_op jit(solution)/shard_map/ppermute | solution.py:15
  25.6 4.4 %collective-permute-start.5 = (bf16[70,3,256]{2,1,0:T(4,128)(2,1)S(1)}, bf16[70,3,256]{2,1,0:T(4,128)(2,1)S(1)}, u32[]{:S(2)}, u32[]{:S(2)}) collective-permute-start(bf16[70,3,256]{2,1,0:T(4,128)(2,1)S(1)} %get-tuple-element.97), channel_id=1, source_target_pairs={{1,0},{2,1},{3,2},{4,3},{5,4},{6,5},{7,6},{8,7},{9,8},{10,9},{11,1... | collective-permute-start | bytes 322568 | tf_op jit(solution)/shard_map/ppermute | solution.py:27
  30.3 2.7 %collective-permute-done.4 = bf16[70,3,256]{2,1,0:T(4,128)(2,1)S(1)} collective-permute-done((bf16[70,3,256]{2,1,0:T(4,128)(2,1)S(1)}, bf16[70,3,256]{2,1,0:T(4,128)(2,1)S(1)}, u32[]{:S(2)}, u32[]{:S(2)}) %collective-permute-start.4) | collective-permute-done | bytes 107552 | tf_op jit(solution)/shard_map/ppermute | solution.py:25
  33.0 1.9 %maximum_convert_fusion = f32[70,38,256]{2,1,0:T(8,128)S(1)} fusion(bf16[70,3,256]{2,1,0:T(4,128)(2,1)S(1)} %collective-permute-done.5, bf16[3,32,256]{2,1,0:T(8,128)(2,1)S(1)} %rev.6, bf16[64,32,256]{2,1,0:T(8,128)(2,1)} %copy-done.4, bf16[3,32,256]{2,1,0:T(8,128)(2,1)S(1)} %broadcast_in_dim.2, bf16[70,3,256]{2,1,0:T(4,128)(2,1)S(1)} %collective-permute-done.4), kind=kLoop, calls=%fused_computation.219 | loop fusion | flops 6809600 | bytes 4085760 | tf_op jit(solution)/shard_map/convert_element_type | solution.py:53
  35.2 15.9 %fusion.115 = (f32[64,32]{1,0:T(8,128)S(1)}, f32[64,32,256]{2,1,0:T(8,128)}) fusion(f32[70,38,256]{2,1,0:T(8,128)S(1)} %maximum_convert_fusion, f32[256]{0:T(256)S(1)} %bitcast.211, f32[256]{0:T(256)S(1)} %bitcast.213, f32[256]{0:T(256)S(1)} %bitcast.119, f32[256]{0:T(256)S(1)} %bitcast.121, f32[256]{0:T(256)S(1)} %bitcast.123, f32[256]{0:T(256)S(1)} %bitcast.125, ...), kind=kLoop, calls=%fused_computation.242 | loop fusion | flops 51378176 | bytes 104915968 | tf_op jit(solution)/shard_map/reduce_sum | solution.py:62
  51.1 2.4 %multiply_reduce_fusion.51 = f32[64,32]{1,0:T(8,128)S(1)} fusion(f32[64,32,256]{2,1,0:T(8,128)} %get-tuple-element.93, f32[64,32]{1,0:T(8,128)S(1)} %broadcast_multiply_fusion.3), kind=kLoop, calls=%fused_computation.216 | loop fusion | flops 1570816 | bytes 2113536 | tf_op jit(solution)/shard_map/reduce_sum | solution.py:64
  55.6 4.2 %fusion.7 = f32[256,1024]{1,0:T(8,128)} fusion(bf16[2048,256]{1,0:T(8,128)(2,1)S(1)} %bitcast.115, f32[2048,1024]{1,0:T(8,128)S(1)} %fusion.121), kind=kOutput, calls=%fused_computation.59 | convolution fusion | flops 1092616192 | bytes 10485760 | tf_op jit(solution)/shard_map/dot_general | solution.py:83
  59.7 6.3 %fusion.6 = bf16[2048,1024]{1,0:T(8,128)(2,1)S(1)} fusion(f32[2048,1024]{1,0:T(8,128)S(1)} %fusion.121, bf16[2048,256]{1,0:T(8,128)(2,1)S(1)} %bitcast.116, bf16[256,1024]{1,0:T(8,128)(2,1)S(1)} %copy-done.87), kind=kOutput, calls=%fused_computation.57 | convolution fusion | flops 1115684864 | bytes 14155776 | tf_op jit(solution)/shard_map/dot_general | solution.py:75
  66.0 2.3 %fusion.122 = f32[256,1024]{1,0:T(8,128)} fusion(bf16[2048,256]{1,0:T(8,128)(2,1)S(1)} %bitcast.114, bf16[2048,1024]{1,0:T(8,128)(2,1)S(1)} %fusion.6), kind=kOutput, calls=%fused_computation.249 | convolution fusion | flops 1073741824 | bytes 6291456 | tf_op jit(solution)/shard_map/dot_general | solution.py:82
  68.3 2.6 %multiply_reduce_fusion.50 = (f32[2048]{0:T(1024)S(1)}, f32[2048,256]{1,0:T(8,128)}) fusion(f32[256]{0:T(256)S(1)} %copy-done.13, bf16[2048,1024]{1,0:T(8,128)(2,1)S(1)} %fusion.6, bf16[256,1024]{1,0:T(8,128)(2,1)S(1)} %copy-done), kind=kOutput, calls=%fused_computation.214 | convolution fusion | flops 1074788352 | bytes 6824960 | tf_op jit(solution)/shard_map/dot_general | solution.py:92
  70.9 2.9 %multiply_reduce_fusion.49 = f32[64,32]{1,0:T(8,128)S(1)} fusion(f32[64,32,256]{2,1,0:T(8,128)} %bitcast.112, f32[64,32,256]{2,1,0:T(8,128)} %get-tuple-element.93, f32[256]{0:T(256)S(1)} %copy-done.13, f32[64,32]{1,0:T(8,128)S(1)} %add_rsqrt_fusion, f32[64,32]{1,0:T(8,128)S(1)} %broadcast_multiply_fusion.3), kind=kLoop, calls=%fused_computation.213 | loop fusion | flops 2619392 | bytes 4219904 | tf_op jit(solution)/shard_map/reduce_sum | solution.py:97
  74.4 6.7 %multiply_reduce_fusion = (f32[256]{0:T(256)}, f32[256]{0:T(256)}, f32[256]{0:T(256)}, f32[256]{0:T(256)}, f32[256]{0:T(256)}, /*index=5*/f32[256]{0:T(256)}, f3...) fusion(f32[70,38,256]{2,1,0:T(8,128)S(1)} %maximum_convert_fusi, ...), kind=kLoop, calls=%fused_computation.163 | loop fusion | flops 22539776 | bytes 44092416 | tf_op jit(solution)/shard_map/reduce_sum | solution.py:103
  81.4 4.5 %multiply_reduce_fusion.36 = (f32[256]{0:T(256)}, f32[256]{0:T(256)}, f32[256]{0:T(256)}, f32[256]{0:T(256)}, f32[256]{0:T(256)}, /*index=5*/f32[256]{0:T(256)},...) fusion(f32[64,32,256]{2,1,0:T(8,128)S(1)} %get-tuple-element.89, ...), kind=kLoop, calls=%fused_computation.199 | loop fusion | flops 13628160 | bytes 29373440 | tf_op jit(solution)/shard_map/reduce_sum | solution.py:103
  86.3 22.8 %fusion.113 = (bf16[70,38,256]{2,1,0:T(8,128)(2,1)}, f32[70,38,256]{2,1,0:T(8,128)}) fusion(f32[256]{0:T(256)S(1)} %bitcast.212, f32[256]{0:T(256)S(1)} %bitcast.214, f32[256]{0:T(256)S(1)} %bitcast.120, f32[256]{0:T(256)S(1)} %bitcast.122, f32[256]{0:T(256)S(1)} %bitcast.124, f32[256]{0:T(256)S(1)} %bitcast.126, f32[256]{0:T(256)S(1)} %bitcast.128, ...), kind=kLoop, calls=%fused_computation.241 | loop fusion | flops 66734080 | bytes 6233088 | tf_op jit(solution)/shard_map/convert.3
  109.2 1.6 maximum_multiply_fusion
  110.7 1.8 fusion.116
  113.2 3.8 %collective-permute-start.7 = (bf16[70,3,256]{2,1,0:T(4,128)(2,1)}, bf16[70,3,256]{2,1,0:T(4,128)(2,1)}, u32[]{:S(2)}, u32[]{:S(2)}) collective-permute-start(bf16[70,3,256]{2,1,0:T(4,128)(2,1)} %get-tuple-element.95), channel_id=1, source_target_pairs={{1,0},{2,1},{3,2},{4,3},{5,4},{6,5},{7,6},{8,7},{9,8},{10,9},{11,1... | collective-permute-start | bytes 322568 | tf_op jit(solution)/shard_map/ppermute | solution.py:27
  117.0 6.6 %multiply_reduce_fusion.18 = (f32[256]{0:T(256)S(1)}, f32[256]{0:T(256)S(1)}, f32[256]{0:T(256)S(1)}, f32[256]{0:T(256)S(1)}, f32[256]{0:T(256)S(1)}, /*index=5*...) fusion(f32[64,32,256]{2,1,0:T(8,128)} %copy-done.3, ...), kind=kLoop, calls=%fused_computation.181 | loop fusion | flops 18869760 | bytes 39864320 | tf_op jit(solution)/shard_map/reduce_sum | solution.py:103
  123.6 5.0 %stack.199 = f32[49,256]{1,0:T(8,128)S(1)} concatenate(f32[1,256]{1,0:T(1,128)} %bitcast.263, f32[1,256]{1,0:T(1,128)} %bitcast.262, f32[1,256]{1,0:T(1,128)} %bitcast.261, f32[1,256]{1,0:T(1,128)} %bitcast.260, f32[1,256]{1,0:T(1,128)} %bitcast.259, f32[1,256]{1,0:T(1,128)} %bitcast.258, f32[1,256]{1,0:T(1,128)} %bitcast.257, f32[1,256]{1,0:T(1,128)} %bitcast.256, ...), dimensions={0} | concatenate | bytes 100352 | tf_op jit(solution)/shard_map/stack | solution.py:109
  128.7 2.3 %slice.866 = f32[70,32,256]{2,1,0:T(8,128)S(1)} slice(f32[70,38,256]{2,1,0:T(8,128)} %get-tuple-element.91), slice={[0:70], [3:35], [0:256]} | slice | bytes 4587520 | tf_op jit(solution)/shard_map/slice | solution.py:138
  132.5 5.9 %scatter-add.10 = f32[70,32,256]{2,1,0:T(8,128)S(1)} dynamic-update-slice(f32[70,32,256]{2,1,0:T(8,128)S(1)} %slice.866, f32[70,3,256]{2,1,0:T(4,128)S(1)} %convert_add_fusion.1, s32[]{:T(128)} %constant.108.clone.1, s32[]{:T(128)} %constant.108.clone.1, s32[]{:T(128)} %constant.108.clone.1) | dynamic-update-slice | bytes 430084 | tf_op jit(solution)/shard_map/scatter-add | solution.py:139
  139.7 4.1 %scatter-add.11 = f32[70,32,256]{2,1,0:T(8,128)S(1)} dynamic-update-slice(f32[70,32,256]{2,1,0:T(8,128)S(1)} %scatter-add.10, f32[70,3,256]{2,1,0:T(4,128)S(1)} %slice_add_fusion, s32[]{:T(128)} %constant.108.clone.1, s32[]{:T(128)} %constant.109.clone.1, s32[]{:T(128)} %constant.108.clone.1) | dynamic-update-slice | bytes 430084 | tf_op jit(solution)/shard_map/scatter-add | solution.py:140
  146.5 2.7 %collective-permute-done.13 = f32[7,7,256]{2,1,0:T(8,128)S(1)} collective-permute-done((f32[7,7,256]{2,1,0:T(8,128)S(1)}, f32[7,7,256]{2,1,0:T(8,128)S(1)}, u32[]{:S(2)}, u32[]{:S(2)}) %collective-permute-start.13) | collective-permute-done | bytes 50208 | tf_op jit(solution)/shard_map/ppermute | solution.py:120
  151.3 5.1 %collective-permute-done.14 = f32[7,7,256]{2,1,0:T(8,128)S(1)} collective-permute-done((f32[7,7,256]{2,1,0:T(8,128)S(1)}, f32[7,7,256]{2,1,0:T(8,128)S(1)}, u32[]{:S(2)}, u32[]{:S(2)}) %collective-permute-start.14) | collective-permute-done | bytes 50208 | tf_op jit(solution)/shard_map/ppermute | solution.py:120
  157.5 1.9 %collective-permute-start.11 = (bf16[3,32,256]{2,1,0:T(8,128)(2,1)S(1)}, bf16[3,32,256]{2,1,0:T(8,128)(2,1)S(1)}, u32[]{:S(2)}, u32[]{:S(2)}) collective-permute-start(bf16[3,32,256]{2,1,0:T(8,128)(2,1)S(1)} %collective-permute-done.10), channel_id=1, source_target_pairs={{0,8},{8,0},{1,9},{9,1},{2,10},{10,2},{3,11},{11,3},{4,12},{12,4},... | collective-permute-start | bytes 147464 | tf_op jit(solution)/shard_map/ppermute | solution.py:15
  163.4 3.2 %fusion.107 = bf16[64,32,256]{2,1,0:T(8,128)(2,1)} fusion(bf16[64,32,256]{2,1,0:T(8,128)(2,1)} %param.16, f32[64,32,256]{2,1,0:T(8,128)} %fusion.108, f32[64,32]{1,0:T(8,128)S(1)} %copy-done.11), kind=kLoop, calls=%fused_computation.161 | loop fusion | flops 2097152 | bytes 4202496 | tf_op jit(solution)/shard_map/convert_element_type | solution.py:151
  166.6 9.8 %reduce-scatter.2.cloned.1.call-done = f32[16,2048]{1,0:T(8,128)} async-done(((f32[256,2048]{1,0:T(8,128)}), f32[16,2048]{1,0:T(8,128)}) %reduce-scatter.2.cloned.1.call-update) | async-done | bytes 131088 | tf_op jit(solution)/shard_map/reduce_scatter | solution.py:84
  176.4 1.5 fusion.117
  (230 shorter events, 23.0 us)
Async XLA Ops:
  7.2 47.1 %copy-start = (bf16[256,1024]{1,0:T(8,128)(2,1)S(1)}, bf16[256,1024]{1,0:T(8,128)(2,1)}, u32[]{:S(2)}) copy-start(bf16[256,1024]{1,0:T(8,128)(2,1)} %param.19) | copy-start | bytes 1572868
  7.2 169.2 %reduce-scatter.2.cloned.1.call-start = ((), (), s32[]{:S(2)}) async-start(), calls=%async_computation.1 | async-start | bytes 2228224 | tf_op jit(solution)/shard_map/reduce_scatter | solution.py:84
  9.8 23.2 %copy-start.4 = (bf16[64,32,256]{2,1,0:T(8,128)(2,1)}, bf16[64,32,256]{2,1,0:T(8,128)(2,1)S(1)}, u32[]{:S(2)}) copy-start(bf16[64,32,256]{2,1,0:T(8,128)(2,1)S(1)} %broadcast_multiply_fusion) | copy-start | bytes 3145732
  9.8 1.4 collective-permute-start
  10.4 22.6 %copy-start.10 = (f32[64,32]{1,0:T(8,128)}, f32[64,32]{1,0:T(8,128)S(1)}, u32[]{:S(2)}) copy-start(f32[64,32]{1,0:T(8,128)S(1)} %copy.14) | copy-start | bytes 24580
  11.2 4.9 %collective-permute-start.1 = (bf16[3,32,256]{2,1,0:T(8,128)(2,1)S(1)}, bf16[3,32,256]{2,1,0:T(8,128)(2,1)S(1)}, u32[]{:S(2)}, u32[]{:S(2)}) collective-permute-start(bf16[3,32,256]{2,1,0:T(8,128)(2,1)S(1)} %collective-permute-done), channel_id=1, source_target_pairs={{0,2},{2,0},{1,3},{3,1},{4,6},{6,4},{5,7},{7,5},{8,10},{10,8},{9,1... | collective-permute-start | bytes 147464 | tf_op jit(solution)/shard_map/ppermute | solution.py:15
  16.1 4.1 %collective-permute-start.2 = (bf16[3,32,256]{2,1,0:T(8,128)(2,1)S(1)}, bf16[3,32,256]{2,1,0:T(8,128)(2,1)S(1)}, u32[]{:S(2)}, u32[]{:S(2)}) collective-permute-start(bf16[3,32,256]{2,1,0:T(8,128)(2,1)S(1)} %collective-permute-done.1), channel_id=1, source_target_pairs={{0,4},{4,0},{1,5},{5,1},{2,6},{6,2},{3,7},{7,3},{8,12},{12,8},{9,1... | collective-permute-start | bytes 147464 | tf_op jit(solution)/shard_map/ppermute | solution.py:15
  18.2 16.6 %copy-start.14 = (f32[1,1,256]{2,1,0:T(1,128)}, f32[1,1,256]{2,1,0:T(1,128)S(1)}, u32[]{:S(2)}) copy-start(f32[1,1,256]{2,1,0:T(1,128)S(1)} %get-tuple-element.113) | copy-start | bytes 3076
  18.2 16.6 %copy-start.16 = (f32[1,1,256]{2,1,0:T(1,128)}, f32[1,1,256]{2,1,0:T(1,128)S(1)}, u32[]{:S(2)}) copy-start(f32[1,1,256]{2,1,0:T(1,128)S(1)} %get-tuple-element.114) | copy-start | bytes 3076
  18.2 16.6 %copy-start.18 = (f32[1,1,256]{2,1,0:T(1,128)}, f32[1,1,256]{2,1,0:T(1,128)S(1)}, u32[]{:S(2)}) copy-start(f32[1,1,256]{2,1,0:T(1,128)S(1)} %get-tuple-element.115) | copy-start | bytes 3076
  18.2 16.6 %copy-start.20 = (f32[1,1,256]{2,1,0:T(1,128)}, f32[1,1,256]{2,1,0:T(1,128)S(1)}, u32[]{:S(2)}) copy-start(f32[1,1,256]{2,1,0:T(1,128)S(1)} %get-tuple-element.116) | copy-start | bytes 3076
  18.2 16.6 %copy-start.22 = (f32[1,1,256]{2,1,0:T(1,128)}, f32[1,1,256]{2,1,0:T(1,128)S(1)}, u32[]{:S(2)}) copy-start(f32[1,1,256]{2,1,0:T(1,128)S(1)} %get-tuple-element.117) | copy-start | bytes 3076
  18.3 16.6 %copy-start.24 = (f32[1,1,256]{2,1,0:T(1,128)}, f32[1,1,256]{2,1,0:T(1,128)S(1)}, u32[]{:S(2)}) copy-start(f32[1,1,256]{2,1,0:T(1,128)S(1)} %get-tuple-element.118) | copy-start | bytes 3076
  20.3 5.1 %collective-permute-start.3 = (bf16[3,32,256]{2,1,0:T(8,128)(2,1)S(1)}, bf16[3,32,256]{2,1,0:T(8,128)(2,1)S(1)}, u32[]{:S(2)}, u32[]{:S(2)}) collective-permute-start(bf16[3,32,256]{2,1,0:T(8,128)(2,1)S(1)} %collective-permute-done.2), channel_id=1, source_target_pairs={{0,8},{8,0},{1,9},{9,1},{2,10},{10,2},{3,11},{11,3},{4,12},{12,4},... | collective-permute-start | bytes 147464 | tf_op jit(solution)/shard_map/ppermute | solution.py:15
  23.9 11.0 %copy-start.30 = (f32[1,1,256]{2,1,0:T(1,128)}, f32[1,1,256]{2,1,0:T(1,128)S(1)}, u32[]{:S(2)}) copy-start(f32[1,1,256]{2,1,0:T(1,128)S(1)} %get-tuple-element.121) | copy-start | bytes 3076
  23.9 11.0 %copy-start.32 = (f32[1,1,256]{2,1,0:T(1,128)}, f32[1,1,256]{2,1,0:T(1,128)S(1)}, u32[]{:S(2)}) copy-start(f32[1,1,256]{2,1,0:T(1,128)S(1)} %get-tuple-element.122) | copy-start | bytes 3076
  23.9 11.0 %copy-start.34 = (f32[1,1,256]{2,1,0:T(1,128)}, f32[1,1,256]{2,1,0:T(1,128)S(1)}, u32[]{:S(2)}) copy-start(f32[1,1,256]{2,1,0:T(1,128)S(1)} %get-tuple-element.123) | copy-start | bytes 3076
  24.0 11.0 %copy-start.36 = (f32[1,1,256]{2,1,0:T(1,128)}, f32[1,1,256]{2,1,0:T(1,128)S(1)}, u32[]{:S(2)}) copy-start(f32[1,1,256]{2,1,0:T(1,128)S(1)} %get-tuple-element.124) | copy-start | bytes 3076
  25.6 7.4 %collective-permute-start.4 = (bf16[70,3,256]{2,1,0:T(4,128)(2,1)S(1)}, bf16[70,3,256]{2,1,0:T(4,128)(2,1)S(1)}, u32[]{:S(2)}, u32[]{:S(2)}) collective-permute-start(bf16[70,3,256]{2,1,0:T(4,128)(2,1)S(1)} %get-tuple-element.96), channel_id=1, source_target_pairs={{0,1},{1,2},{2,3},{3,4},{4,5},{5,6},{6,7},{7,8},{8,9},{9,10},{10,1... | collective-permute-start | bytes 322568 | tf_op jit(solution)/shard_map/ppermute | solution.py:25
  25.6 7.3 %collective-permute-start.5 = (bf16[70,3,256]{2,1,0:T(4,128)(2,1)S(1)}, bf16[70,3,256]{2,1,0:T(4,128)(2,1)S(1)}, u32[]{:S(2)}, u32[]{:S(2)}) collective-permute-start(bf16[70,3,256]{2,1,0:T(4,128)(2,1)S(1)} %get-tuple-element.97), channel_id=1, source_target_pairs={{1,0},{2,1},{3,2},{4,3},{5,4},{6,5},{7,6},{8,7},{9,8},{10,9},{11,1... | collective-permute-start | bytes 322568 | tf_op jit(solution)/shard_map/ppermute | solution.py:27
  86.3 22.9 %copy-start.8 = (f32[256,1024]{1,0:T(8,128)S(1)}, f32[256,1024]{1,0:T(8,128)}, u32[]{:S(2)}) copy-start(f32[256,1024]{1,0:T(8,128)} %fusion.7) | copy-start | bytes 3145732
  86.3 22.9 %copy-start.9 = (f32[256,1024]{1,0:T(8,128)S(1)}, f32[256,1024]{1,0:T(8,128)}, u32[]{:S(2)}) copy-start(f32[256,1024]{1,0:T(8,128)} %fusion.122) | copy-start | bytes 3145732
  112.6 18.4 %collective-permute-start.6 = (bf16[70,3,256]{2,1,0:T(4,128)(2,1)S(1)}, bf16[70,3,256]{2,1,0:T(4,128)(2,1)}, u32[]{:S(2)}, u32[]{:S(2)}) collective-permute-start(bf16[70,3,256]{2,1,0:T(4,128)(2,1)S(1)} %get-tuple-element.94), channel_id=1, source_target_pairs={{0,1},{1,2},{2,3},{3,4},{4,5},{5,6},{6,7},{7,8},{8,9},{9,10},{10,1... | collective-permute-start | bytes 322568 | tf_op jit(solution)/shard_map/ppermute | solution.py:25
  113.2 17.8 %collective-permute-start.7 = (bf16[70,3,256]{2,1,0:T(4,128)(2,1)}, bf16[70,3,256]{2,1,0:T(4,128)(2,1)}, u32[]{:S(2)}, u32[]{:S(2)}) collective-permute-start(bf16[70,3,256]{2,1,0:T(4,128)(2,1)} %get-tuple-element.95), channel_id=1, source_target_pairs={{1,0},{2,1},{3,2},{4,3},{5,4},{6,5},{7,6},{8,7},{9,8},{10,9},{11,1... | collective-permute-start | bytes 322568 | tf_op jit(solution)/shard_map/ppermute | solution.py:27
  128.6 15.7 %collective-permute-start.12 = (f32[7,7,256]{2,1,0:T(8,128)S(1)}, f32[7,7,256]{2,1,0:T(8,128)S(1)}, u32[]{:S(2)}, u32[]{:S(2)}) collective-permute-start(f32[7,7,256]{2,1,0:T(8,128)S(1)} %mul.1497), channel_id=1, source_target_pairs={{0,1},{1,0},{2,3},{3,2},{4,5},{5,4},{6,7},{7,6},{8,9},{9,8},{10,11... | collective-permute-start | bytes 150536 | tf_op jit(solution)/shard_map/ppermute | solution.py:120
  143.8 1.4 collective-permute-start.8
  144.4 4.8 %collective-permute-start.13 = (f32[7,7,256]{2,1,0:T(8,128)S(1)}, f32[7,7,256]{2,1,0:T(8,128)S(1)}, u32[]{:S(2)}, u32[]{:S(2)}) collective-permute-start(f32[7,7,256]{2,1,0:T(8,128)S(1)} %add.452), channel_id=1, source_target_pairs={{0,2},{1,3},{2,0},{3,1},{4,6},{5,7},{6,4},{7,5},{8,10},{9,11},{10,... | collective-permute-start | bytes 150536 | tf_op jit(solution)/shard_map/ppermute | solution.py:120
  145.3 4.6 %collective-permute-start.9 = (bf16[3,32,256]{2,1,0:T(8,128)(2,1)S(1)}, bf16[3,32,256]{2,1,0:T(8,128)(2,1)S(1)}, u32[]{:S(2)}, u32[]{:S(2)}) collective-permute-start(bf16[3,32,256]{2,1,0:T(8,128)(2,1)S(1)} %collective-permute-done.8), channel_id=1, source_target_pairs={{0,2},{2,0},{1,3},{3,1},{4,6},{6,4},{5,7},{7,5},{8,10},{10,8},{9,1... | collective-permute-start | bytes 147464 | tf_op jit(solution)/shard_map/ppermute | solution.py:15
  149.2 7.2 %collective-permute-start.14 = (f32[7,7,256]{2,1,0:T(8,128)S(1)}, f32[7,7,256]{2,1,0:T(8,128)S(1)}, u32[]{:S(2)}, u32[]{:S(2)}) collective-permute-start(f32[7,7,256]{2,1,0:T(8,128)S(1)} %add.453), channel_id=1, source_target_pairs={{0,4},{1,5},{2,6},{3,7},{4,0},{5,1},{6,2},{7,3},{8,12},{9,13},{10,... | collective-permute-start | bytes 150536 | tf_op jit(solution)/shard_map/ppermute | solution.py:120
  149.9 7.7 %collective-permute-start.10 = (bf16[3,32,256]{2,1,0:T(8,128)(2,1)S(1)}, bf16[3,32,256]{2,1,0:T(8,128)(2,1)S(1)}, u32[]{:S(2)}, u32[]{:S(2)}) collective-permute-start(bf16[3,32,256]{2,1,0:T(8,128)(2,1)S(1)} %collective-permute-done.9), channel_id=1, source_target_pairs={{0,4},{4,0},{1,5},{5,1},{2,6},{6,2},{3,7},{7,3},{8,12},{12,8},{9,1... | collective-permute-start | bytes 147464 | tf_op jit(solution)/shard_map/ppermute | solution.py:15
  156.4 5.5 %collective-permute-start.15 = (f32[7,7,256]{2,1,0:T(8,128)S(1)}, f32[7,7,256]{2,1,0:T(8,128)S(1)}, u32[]{:S(2)}, u32[]{:S(2)}) collective-permute-start(f32[7,7,256]{2,1,0:T(8,128)S(1)} %add.454), channel_id=1, source_target_pairs={{0,8},{1,9},{2,10},{3,11},{4,12},{5,13},{6,14},{7,15},{8,0},{9,1},... | collective-permute-start | bytes 150536 | tf_op jit(solution)/shard_map/ppermute | solution.py:120
  157.5 5.1 %collective-permute-start.11 = (bf16[3,32,256]{2,1,0:T(8,128)(2,1)S(1)}, bf16[3,32,256]{2,1,0:T(8,128)(2,1)S(1)}, u32[]{:S(2)}, u32[]{:S(2)}) collective-permute-start(bf16[3,32,256]{2,1,0:T(8,128)(2,1)S(1)} %collective-permute-done.10), channel_id=1, source_target_pairs={{0,8},{8,0},{1,9},{9,1},{2,10},{10,2},{3,11},{11,3},{4,12},{12,4},... | collective-permute-start | bytes 147464 | tf_op jit(solution)/shard_map/ppermute | solution.py:15
  (73 other events, 385.5 us)
Sparse Core Ops, SparseCore 0:
  110.9 65.4 reduce-scatter.1
